TPU v7x, 32 devices: a whole 2x2x4 slice. The times are simulated.
32 devices in a mesh: grp: 2 (over x), scan: 8 (over z, y), det: 2 (over core).
Axes of the slice: x: 2, y: 2, z: 4, core: 2. Of those that a mesh axis runs over, the one named last changes fastest.
Arguments:
- spectra: float32 [16384, 4096], P(('grp', 'scan'), 'det'), parts along dimension 0, may hold values from 0 to 544, as said below
- basis: float32 [64, 4096], P('grp', 'det'), parts along dimension 0, may hold values from 0.03 to 8, as said below
- loadings: float32 [64, 8192], P('grp', 'scan'), parts along dimension 0, may hold values from 0.005 to 6, as said below
Outputs:
- new_loadings: float32 [64, 8192], P('grp', 'scan'), parts along dimension 0
- new_basis: float32 [64, 4096], P('grp', 'det'), parts along dimension 0
There are 2 independent parts, one for each index of `grp`. A program takes and returns all parts, laid end to end along the dimension named above; each array names one. Nothing has to cross between parts.
Inputs may be any that keep to these rules, and one draw needn't show every extreme that they name: `spectra`: intensities are nonnegative. `basis`: entries are positive. `loadings`: entries are positive.
All inputs are finite; a program needn't handle non-finite values.
Results may differ from a plain program's by a relative error of at most 0.00005.
Values sent between devices are 32-bit elements; how exact they have to be, the bound alone decides.
A program may use at most 64 MiB of HBM per device.

v0:
```python
import jax
import jax.numpy as jnp
from jax import lax
from jax.sharding import PartitionSpec as P

HIGHEST = lax.Precision.HIGHEST


def swapped(block, axis, stride):
    count = lax.axis_size(axis)
    route = []
    for low in range(count):
        high = low | 1 << stride
        if high != low and high < count:
            route += [(low, high), (high, low)]
    return lax.ppermute(block, axis, route)


def per_device(spectra, basis, loadings):
    partner = swapped(basis, "det", 0)
    tied = 0.5 * (basis + jnp.flip(partner, 1))
    local_numer = lax.dot_general(tied, spectra, (((1,), (1,)), ((), ())), precision=HIGHEST)
    gram = 2.0 * lax.dot_general(tied, tied, (((1,), (1,)), ((), ())), precision=HIGHEST)
    numer_h = lax.psum(local_numer, "det")
    new_loadings = loadings * numer_h / jnp.dot(gram, loadings, precision=HIGHEST)
    w_terms = jnp.dot(new_loadings, spectra, precision=HIGHEST)
    cross_terms = lax.dot_general(
        new_loadings, new_loadings, (((1,), (1,)), ((), ())), precision=HIGHEST
    )
    numer_w, cross = lax.psum((w_terms, cross_terms), "scan")
    mirrored = swapped(numer_w, "det", 0)
    tied_numer = 0.5 * (numer_w + jnp.flip(mirrored, 1))
    new_basis = tied * tied_numer / jnp.dot(cross, tied, precision=HIGHEST)
    return (new_loadings, new_basis)


def solution(mesh):
    in_specs = (P(("grp", "scan"), "det"), P("grp", "det"), P("grp", "scan"))
    out_specs = (P("grp", "scan"), P("grp", "det"))
    return jax.shard_map(
        per_device, mesh=mesh, in_specs=in_specs, out_specs=out_specs, check_vma=False
    )
```

profile of v0, /device:TPU:0, one launch (start us, length us, event | category | flops | bytes accessed | tf_op | source)
XLA Modules:
  0.0 169.7 jit_solution(7217789478776410331)
XLA Ops:
  7.2 0.0 copy-start.1
  7.2 0.0 all-reduce.3.cloned.1.call-start
  7.2 0.6 collective-permute-start
  7.8 1.4 collective-permute-done
  9.2 1.2 rev.7
  10.3 1.0 add_multiply_fusion
  11.3 10.6 %fusion = f32[32,1024]{1,0:T(8,128)} fusion(f32[32,2048]{1,0:T(8,128)S(1)} %add_multiply_fusion, f32[1024,2048]{1,0:T(8,128)} %param.3), kind=kOutput, calls=%fused_computation.4 | convolution fusion | flops 805306368 | bytes 8781824 | tf_op jit(solution)/shard_map/dot_general | solution.py:22
  21.9 0.0 all-reduce.3.cloned.1.call-update
  21.9 0.0 all-reduce.5.cloned.1.call-start
  22.0 0.3 convolution_multiply_fusion
  22.3 20.3 %all-reduce.3.cloned.1.call-done = f32[32,1024]{1,0:T(8,128)} async-done(((f32[32,1024]{1,0:T(8,128)}), f32[32,1024]{1,0:T(8,128)}) %all-reduce.3.cloned.1.call-update) | async-done | bytes 131088 | tf_op jit(solution)/shard_map/psum | solution.py:24
  42.6 0.0 copy-done.1
  42.6 1.2 convolution_divide_fusion
  43.8 0.0 copy-start
  43.8 7.9 %fusion.1 = f32[32,2048]{1,0:T(8,128)} fusion(f32[32,1024]{1,0:T(8,128)S(1)} %convolution_divide_fusion, f32[1024,2048]{1,0:T(8,128)} %param.3), kind=kOutput, calls=%fused_computation.5 | convolution fusion | flops 805306368 | bytes 8781824 | tf_op jit(solution)/shard_map/dot_general | solution.py:26
  51.7 0.0 all-reduce.5.cloned.1.call-update
  51.7 72.4 %all-reduce.5.cloned.1.call-done = f32[32,2048]{1,0:T(8,128)} async-done(((f32[32,2048]{1,0:T(8,128)}), f32[32,2048]{1,0:T(8,128)}) %all-reduce.5.cloned.1.call-update) | async-done | bytes 262160 | tf_op jit(solution)/shard_map/psum | solution.py:30
  124.1 0.0 collective-permute-start.1
  124.1 0.2 fusion.2
  124.3 35.3 %psum.23 = f32[32,32]{1,0:T(8,128)S(1)} all-reduce(f32[32,32]{1,0:T(8,128)S(1)} %fusion.2), channel_id=1, replica_groups=mesh['grp'=2,'scan'=8,'det'=2] {'scan'}, use_global_device_ids=true, to_apply=%region_2.3 | all-reduce | flops 1024 | bytes 8192 | tf_op jit(solution)/shard_map/psum | solution.py:30
  159.7 0.0 collective-permute-done.1
  159.7 1.2 rev.8
  160.8 2.0 %multiply_divide_fusion = f32[32,2048]{1,0:T(8,128)} fusion(f32[32,2048]{1,0:T(8,128)S(1)} %add_multiply_fusion, f32[32,2048]{1,0:T(8,128)} %all-reduce.5.cloned.1.call-done, f32[32,2048]{1,0:T(8,128)S(1)} %rev.8, f32[32,32]{1,0:T(8,128)S(1)} %psum.23), kind=kOutput, calls=%fused_computation.2 | convolution fusion | flops 25427968 | bytes 1052672 | tf_op jit(solution)/shard_map/dot_general | solution.py:33
  162.9 0.0 copy-done
Async XLA Ops:
  7.2 35.4 %copy-start.1 = (f32[32,1024]{1,0:T(8,128)S(1)}, f32[32,1024]{1,0:T(8,128)}, u32[]{:S(2)}) copy-start(f32[32,1024]{1,0:T(8,128)} %param.5) | copy-start | bytes 393220
  7.2 35.4 %all-reduce.3.cloned.1.call-start = ((), (), s32[]{:S(2)}) async-start(), calls=%async_computation | async-start | bytes 262144 | tf_op jit(solution)/shard_map/psum | solution.py:24
  7.2 1.9 %collective-permute-start = (f32[32,2048]{1,0:T(8,128)}, f32[32,2048]{1,0:T(8,128)S(1)}, u32[]{:S(2)}, u32[]{:S(2)}) collective-permute-start(f32[32,2048]{1,0:T(8,128)} %param.4), channel_id=1, source_target_pairs={{0,1},{1,0},{2,3},{3,2},{4,5},{5,4},{6,7},{7,6},{8,9},{9,8},{10,11... | collective-permute-start | bytes 786440 | tf_op jit(solution)/shard_map/ppermute | solution.py:16
  21.9 102.2 %all-reduce.5.cloned.1.call-start = ((), (), s32[]{:S(2)}) async-start(), calls=%async_computation.1 | async-start | bytes 524288 | tf_op jit(solution)/shard_map/psum | solution.py:30
  43.8 119.1 %copy-start = (f32[32,1024]{1,0:T(8,128)}, f32[32,1024]{1,0:T(8,128)S(1)}, u32[]{:S(2)}) copy-start(f32[32,1024]{1,0:T(8,128)S(1)} %convolution_divide_fusion) | copy-start | bytes 393220
  124.1 35.6 %collective-permute-start.1 = (f32[32,2048]{1,0:T(8,128)}, f32[32,2048]{1,0:T(8,128)S(1)}, u32[]{:S(2)}, u32[]{:S(2)}) collective-permute-start(f32[32,2048]{1,0:T(8,128)} %all-reduce.5.cloned.1.call-done), channel_id=1, source_target_pairs={{0,1},{1,0},{2,3},{3,2},{4,5},{5,4},{6,7},{7,6},{8,9},{9,8},{10,11... | collective-permute-start | bytes 786440 | tf_op jit(solution)/shard_map/ppermute | solution.py:16
Sparse Core Ops, SparseCore 0:
  22.0 20.5 all-reduce.2
  51.8 72.1 all-reduce.4
where the time goes:
time: 170 us
  waiting for transfers between devices  94 us (55%)
  blocking collectives  35.3 us (21%)
  matrix products  22.3 us (13%)
  between operations  14.1 us (8%)
  local copies, waits for them, and re-layouts  2.34 us (1%)
    psum x1, waiting for transfers between devices, per_device(): numer_w, cross = lax.psum((w_terms, cross_terms), 'scan')  72.4 us
    psum x1, blocking collectives, per_device(): numer_w, cross = lax.psum((w_terms, cross_terms), 'scan')  35.3 us
    psum x1, waiting for transfers between devices, per_device(): numer_h = lax.psum(local_numer, 'det')  20.3 us
    dot_general x1, matrix products, per_device(): lax.dot_general(tied, spectra, (((1,), (1,)), ((), ())), precision=HIGHEST)  10.6 us
    dot_general x1, matrix products, per_device(): w_terms = jnp.dot(new_loadings, spectra, precision=HIGHEST)  7.91 us
  transfers between devices with their start and end apart: 4, of which 3 were waited for; matrix products, arithmetic and copies ran while one was open for 0% of the time, Pallas kernels for 0%

commit v1 on v0

v1 whole, which is shorter than its diff:
```python
import functools

import jax
import jax.numpy as jnp
from jax import lax
from jax.experimental import pallas as pl
from jax.experimental.pallas import tpu as pltpu
from jax.sharding import PartitionSpec as P

HIGHEST = lax.Precision.HIGHEST
MESH = pl.DeviceIdType.MESH
F32 = jnp.float32
BF16 = jnp.bfloat16
LANES = 128


def split(x):
    hi = x.astype(BF16)
    lo = (x - hi.astype(F32)).astype(BF16)
    return hi, lo


def dot_nt(a, b):
    return lax.dot_general(a, b, (((1,), (1,)), ((), ())), preferred_element_type=F32)


def dot_nn(a, b):
    return lax.dot_general(a, b, (((1,), (0,)), ((), ())), preferred_element_type=F32)


def mirrored(x):
    index = (LANES - 1) - lax.broadcasted_iota(jnp.int32, x.shape, 1)
    return jnp.take_along_axis(x, index, axis=1, mode="promise_in_bounds")


def kernel(
    n, load_chunks, pos_chunk, col_chunk, barrier_at,
    spectra, basis, loadings, new_loadings, new_basis,
    sbuf, s_hi, s_lo, own, other, load, tied3, tied2, num_out, num_in, nl2,
    w_keep, w_out, w_in, rs_in, cr_out, cr_in, piece_buf, ag_in, fw_in,
    sp_sem, io_sem, bs_sem, nm_sem, w_sem, rs_send, rs_recv, cr_send, cr_recv,
    ag_send, ag_recv, fw_send, fw_recv,
):
    rank, pixels = basis.shape
    positions = loadings.shape[1]
    blocks = pixels // LANES
    half = blocks // 2
    if n <= half:
        per, row_split = half // n, 1
    else:
        per, row_split = 1, min(n // half, rank // 8)
    owners = half // per * row_split
    rows = rank // row_split
    pack = LANES // rank
    me = lax.axis_index("scan")
    det = lax.axis_index("det")
    partner = {"det": 1 - det}

    def peer(k):
        return lax.rem(me + k, n)

    def source(k):
        return lax.rem(me + n - k, n)

    def owner_only(index, fn):
        if owners == n:
            fn()
        else:
            pl.when(index < owners)(fn)

    def piece_at(index):
        first = index // row_split * per
        row = pl.multiple_of(lax.rem(index, row_split) * rows, 8) if row_split > 1 else 0
        return pl.ds(first, per), pl.ds(row, rows)

    def remote(src, dst, send, recv, where):
        return pltpu.make_async_remote_copy(
            src_ref=src, dst_ref=dst, send_sem=send, recv_sem=recv,
            device_id=where, device_id_type=MESH,
        )

    barrier = pltpu.get_barrier_semaphore()
    pl.semaphore_signal(barrier, inc=1, device_id=partner, device_id_type=MESH)
    for k in range(1, n):
        pl.semaphore_signal(barrier, inc=1, device_id={"scan": peer(k)}, device_id_type=MESH)

    own_copy = pltpu.make_async_copy(basis, own, io_sem.at[0])
    own_copy.start()
    load_rows = positions // load_chunks
    spectra_copies = []
    for i in range(load_chunks):
        part = pl.ds(i * load_rows, load_rows)
        spectra_copies.append(
            pltpu.make_async_copy(spectra.at[part], sbuf.at[part], sp_sem.at[i])
        )
        spectra_copies[i].start()
    load_copy = pltpu.make_async_copy(loadings, load, io_sem.at[1])
    load_copy.start()

    basis_copy = remote(own, other, bs_sem.at[0], bs_sem.at[1], partner)

    def enter():
        own_copy.wait()
        pl.semaphore_wait(barrier, n)
        basis_copy.start()

    for i in range(load_chunks):
        if i == barrier_at:
            enter()
        spectra_copies[i].wait()

        @pl.loop(0, load_rows // 16)
        def _(j):
            part = pl.ds(pl.multiple_of(i * load_rows + j * 16, 16), 16)
            hi, lo = split(sbuf[part, :])
            s_hi[part, :] = hi
            s_lo[part, :] = lo

    if barrier_at >= load_chunks:
        enter()

    basis_copy.wait()
    for b in range(blocks):
        mine = own[:, b * LANES:(b + 1) * LANES]
        back = blocks - 1 - b
        tied = 0.5 * (mine + mirrored(other[:, back * LANES:(back + 1) * LANES]))
        tied3[b] = tied
        hi, lo = split(tied)
        tied2[:rank, b * LANES:(b + 1) * LANES] = hi
        tied2[rank:, b * LANES:(b + 1) * LANES] = lo

    num_copies = []
    for i in range(positions // pos_chunk):
        part = pl.ds(i * pos_chunk, pos_chunk)
        both = dot_nt(tied2[...], s_hi[part, :])
        low = dot_nt(tied2[:rank, :], s_lo[part, :])
        num_out[i] = both[:rank] + (both[rank:] + low)
        num_copies.append(
            remote(num_out.at[i], num_in.at[i], nm_sem.at[0, i], nm_sem.at[1, i], partner)
        )
        num_copies[i].start()

    squares = dot_nt(tied2[...], tied2[...])
    gram = 2.0 * (
        squares[:rank, :rank] + (squares[:rank, rank:] + squares[rank:, :rank])
    )
    load_copy.wait()
    weighted = jnp.dot(gram, load[...], precision=HIGHEST, preferred_element_type=F32)

    for i in range(positions // pos_chunk):
        num_copies[i].wait()
        cols = slice(i * pos_chunk, (i + 1) * pos_chunk)
        fresh = load[:, cols] * (num_out[i] + num_in[i]) / weighted[:, cols]
        new_loadings[:, cols] = fresh
        hi, lo = split(fresh)
        nl2[:rank, cols] = hi
        nl2[rank:, cols] = lo

    squares = dot_nt(nl2[...], nl2[...])
    cross = squares[:rank, :rank] + (squares[:rank, rank:] + squares[rank:, :rank])
    cr_out[...] = jnp.concatenate(
        [cross[i * (rank // pack):(i + 1) * (rank // pack)] for i in range(pack)], axis=1
    )
    cr_copies = [None]
    for k in range(1, n):
        cr_copies.append(
            remote(cr_out, cr_in.at[k], cr_send.at[k], cr_recv.at[k], {"scan": peer(k)})
        )
        cr_copies[k].start()

    def sums(cols):
        both = dot_nn(nl2[...], s_hi[:, cols])
        low = dot_nn(nl2[:rank, :], s_lo[:, cols])
        return both[:rank] + (both[rank:] + low)

    step = col_chunk // LANES
    w_copies = []
    for i in range(half // step):
        first = half + i * step
        value = sums(slice(first * LANES, (first + step) * LANES))
        for j in range(step):
            w_out[i * step + j] = value[:, j * LANES:(j + 1) * LANES]
        part = pl.ds(i * step, step)
        w_copies.append(
            remote(w_out.at[part], w_in.at[part], w_sem.at[0, i], w_sem.at[1, i], partner)
        )
        w_copies[i].start()
    for i in range(half // step):
        value = sums(slice(i * col_chunk, (i + 1) * col_chunk))
        for j in range(step):
            w_keep[i * step + j] = value[:, j * LANES:(j + 1) * LANES]
    for copy in w_copies:
        copy.wait()
    for b in range(half):
        w_keep[b] = w_keep[b] + mirrored(w_in[half - 1 - b])

    rs_copies = [None]
    for k in range(1, n):
        rs_copies.append(
            remote(
                w_keep.at[piece_at(peer(k))], rs_in.at[k], rs_send.at[k], rs_recv.at[k],
                {"scan": peer(k)},
            )
        )
        owner_only(peer(k), rs_copies[k].start)

    for k in range(1, n):
        cr_copies[k].wait()
    packed = cr_out[...]
    for k in range(1, n):
        packed = packed + cr_in[k]
    cross = jnp.concatenate(
        [packed[:, i * rank:(i + 1) * rank] for i in range(pack)], axis=0
    )

    ag_copies = [None]
    for k in range(1, n):
        ag_copies.append(
            remote(piece_buf, ag_in.at[k], ag_send.at[k], ag_recv.at[k], {"scan": peer(k)})
        )
    fw_copies = [remote(piece_buf, fw_in.at[0], fw_send.at[0], fw_recv.at[0], partner)]
    for k in range(1, n):
        fw_copies.append(
            remote(ag_in.at[k], fw_in.at[k], fw_send.at[k], fw_recv.at[k], partner)
        )

    def own_piece():
        first, row = piece_at(me)
        for j in range(per):
            weights = jnp.dot(
                cross, tied3[first.start + j], precision=HIGHEST, preferred_element_type=F32
            )
            if row_split > 1:
                piece_buf[0] = weights[:rows]
                for i in range(1, row_split):
                    @pl.when(lax.rem(me, row_split) == i)
                    def _():
                        piece_buf[0] = weights[i * rows:(i + 1) * rows]
            else:
                piece_buf[j] = weights
        for k in range(1, n):
            rs_copies[k].wait_recv()
        for j in range(per):
            total = w_keep[first.start + j, row, :]
            for k in range(1, n):
                total = total + rs_in[k, j]
            piece_buf[j] = tied3[first.start + j, row, :] * (0.5 * total) / piece_buf[j]
        for k in range(1, n):
            ag_copies[k].start()
        fw_copies[0].start()

    owner_only(me, own_piece)

    def put(index, ref, flip):
        first, row = piece_at(index)
        for j in range(per):
            block = first.start + j
            value = ref[j]
            if flip:
                block = blocks - 1 - block
                value = mirrored(value)
            col = pl.multiple_of(block * LANES, LANES)
            new_basis[row, pl.ds(col, LANES)] = value

    def arrived(k):
        def go():
            ag_copies[k].wait_recv()
            fw_copies[k].start()
            put(source(k), ag_in.at[k], False)
        return go

    def passed_on(k):
        def go():
            fw_copies[k].wait_recv()
            put(source(k), fw_in.at[k], True)
        return go

    for k in range(1, n):
        owner_only(source(k), arrived(k))
    owner_only(me, lambda: put(me, piece_buf, False))
    owner_only(me, passed_on(0))
    for k in range(1, n):
        owner_only(source(k), passed_on(k))

    for k in range(1, n):
        owner_only(peer(k), rs_copies[k].wait_send)
        owner_only(me, ag_copies[k].wait_send)
        owner_only(source(k), fw_copies[k].wait_send)
    owner_only(me, fw_copies[0].wait_send)


def per_device(n, spectra, basis, loadings):
    rank, pixels = basis.shape
    positions = loadings.shape[1]
    blocks = pixels // LANES
    half = blocks // 2
    if n <= half:
        per, row_split = half // n, 1
    else:
        per, row_split = 1, min(n // half, rank // 8)
    rows = rank // row_split
    load_chunks = 8
    pos_chunk = 256
    col_chunk = 256
    pack = LANES // rank
    dma = pltpu.SemaphoreType.DMA
    any_space = pl.BlockSpec(memory_space=pl.ANY)
    vmem = pl.BlockSpec(memory_space=pltpu.VMEM)
    return pl.pallas_call(
        functools.partial(kernel, n, load_chunks, pos_chunk, col_chunk, 4),
        out_shape=(
            jax.ShapeDtypeStruct(loadings.shape, F32),
            jax.ShapeDtypeStruct(basis.shape, F32),
        ),
        in_specs=[any_space] * 3,
        out_specs=(vmem, vmem),
        scratch_shapes=[
            pltpu.VMEM(spectra.shape, F32),
            pltpu.VMEM(spectra.shape, BF16),
            pltpu.VMEM(spectra.shape, BF16),
            pltpu.VMEM((rank, pixels), F32),
            pltpu.VMEM((rank, pixels), F32),
            pltpu.VMEM((rank, positions), F32),
            pltpu.VMEM((blocks, rank, LANES), F32),
            pltpu.VMEM((2 * rank, pixels), BF16),
            pltpu.VMEM((positions // pos_chunk, rank, pos_chunk), F32),
            pltpu.VMEM((positions // pos_chunk, rank, pos_chunk), F32),
            pltpu.VMEM((2 * rank, positions), BF16),
            pltpu.VMEM((half, rank, LANES), F32),
            pltpu.VMEM((half, rank, LANES), F32),
            pltpu.VMEM((half, rank, LANES), F32),
            pltpu.VMEM((n, per, rows, LANES), F32),
            pltpu.VMEM((rank // pack, LANES), F32),
            pltpu.VMEM((n, rank // pack, LANES), F32),
            pltpu.VMEM((per, rows, LANES), F32),
            pltpu.VMEM((n, per, rows, LANES), F32),
            pltpu.VMEM((n, per, rows, LANES), F32),
            dma((load_chunks,)),
            dma((2,)),
            dma((2,)),
            dma((2, positions // pos_chunk)),
            dma((2, half * LANES // col_chunk)),
            dma((n,)), dma((n,)), dma((n,)), dma((n,)),
            dma((n,)), dma((n,)), dma((n,)), dma((n,)),
        ],
        compiler_params=pltpu.CompilerParams(collective_id=0, has_side_effects=True),
        name="nmf_update",
    )(spectra, basis, loadings)


def solution(mesh):
    in_specs = (P(("grp", "scan"), "det"), P("grp", "det"), P("grp", "scan"))
    out_specs = (P("grp", "scan"), P("grp", "det"))
    return jax.shard_map(
        functools.partial(per_device, mesh.shape["scan"]),
        mesh=mesh, in_specs=in_specs, out_specs=out_specs, check_vma=False,
    )
```

time: 170 us -> 32.9 us (0.19)
  waiting for transfers between devices: 94 us -> 0 us
  blocking collectives: 35.3 us -> 0 us
  Pallas kernels: 0 us -> 28.6 us
  matrix products: 22.3 us -> 0 us
  between operations: 14.1 us -> 0.64 us
    psum x2 -> x0, waiting for transfers between devices: 92.6 us -> none  [the longest x1 72.4 us: per_device(): numer_w, cross = lax.psum((w_terms, cross_terms), 'scan')]
    psum x1 -> x0, blocking collectives: 35.3 us -> none  [per_device(): numer_w, cross = lax.psum((w_terms, cross_terms), 'scan')]
    pallas_call x0 -> x1, Pallas kernels: none -> 28.6 us  [per_device(): pl.pallas_call(functools.partial(kernel, n, load_chunks, pos_chunk, col_c...]
    dot_general x6 -> x0, matrix products: 22.3 us -> none  [the longest x1 10.6 us: per_device(): lax.dot_general(tied, spectra, (((1,), (1,)), ((), ())), precision=HIGHEST)]
    unnamed x4 -> x2, local copies, waits for them, and re-layouts: 0.01 us -> 3.24 us
    rev x2 -> x0, local copies, waits for them, and re-layouts: 2.33 us -> none  [the longest x1 1.17 us: per_device(): tied_numer = 0.5 * (numer_w + jnp.flip(mirrored, 1))]
  transfers between devices with their start and end apart: 4 -> 0, of which waited for: 3 -> 0; matrix products, arithmetic and copies ran while one was open for 0% -> 0% of each run, Pallas kernels for 0% -> 0%
where the time goes in v1:
time: 32.9 us; the launch traced here: 32.4 us
  Pallas kernels  28.6 us (87%)
  local copies, waits for them, and re-layouts  3.24 us (10%)
  between operations  0.64 us (2%)
    pallas_call x1, Pallas kernels, per_device(): pl.pallas_call(functools.partial(kernel, n, load_chunks, pos_chunk, col_c...  28.6 us
    unnamed x2, local copies, waits for them, and re-layouts  3.24 us

profile of v1, /device:TPU:0, one launch (start us, length us, event | category | flops | bytes accessed | tf_op | source)
XLA Modules:
  0.0 32.4 jit_solution(4005984202915848586)
XLA Ops:
  0.6 28.6 %nmf_update.1 = (f32[32,1024]{1,0:T(8,128)}, f32[32,2048]{1,0:T(8,128)}) custom-call(f32[1024,2048]{1,0:T(8,128)} %spectra.1, f32[32,2048]{1,0:T(8,128)} %basis.1, f32[32,1024]{1,0:T(8,128)} %loadings.1), custom_call_target="tpu_custom_call" | custom-call | tf_op jit(solution)/shard_map/nmf_update/pallas_call | solution.py:309
  29.2 1.6 %copy.7 = f32[32,1024]{1,0:T(8,128)} copy(f32[32,1024]{1,0:T(8,128)} %get-tuple-element.4) | data formatting | bytes 262144
  30.8 1.7 %copy.8 = f32[32,2048]{1,0:T(8,128)} copy(f32[32,2048]{1,0:T(8,128)} %get-tuple-element.5) | data formatting | bytes 524288

commit v2 on v1

v2 whole, which is shorter than its diff:
```python
import functools

import jax
import jax.numpy as jnp
from jax import lax
from jax.experimental import pallas as pl
from jax.experimental.pallas import tpu as pltpu
from jax.sharding import PartitionSpec as P

HIGHEST = lax.Precision.HIGHEST
MESH = pl.DeviceIdType.MESH
F32 = jnp.float32
BF16 = jnp.bfloat16
LANES = 128


def split(x):
    hi = x.astype(BF16)
    lo = (x - hi.astype(F32)).astype(BF16)
    return hi, lo


def dot_nt(a, b):
    return lax.dot_general(a, b, (((1,), (1,)), ((), ())), preferred_element_type=F32)


def dot_nn(a, b):
    return lax.dot_general(a, b, (((1,), (0,)), ((), ())), preferred_element_type=F32)


def mirrored(x):
    index = (LANES - 1) - lax.broadcasted_iota(jnp.int32, x.shape, 1)
    return jnp.take_along_axis(x, index, axis=1, mode="promise_in_bounds")


def remote(src, dst, send, recv, where):
    return pltpu.make_async_remote_copy(
        src_ref=src, dst_ref=dst, send_sem=send, recv_sem=recv,
        device_id=where, device_id_type=MESH,
    )


def layout(n, rank, pixels):
    half = pixels // LANES // 2
    if n <= half:
        per, row_split = half // n, 1
    else:
        per, row_split = 1, min(n // half, rank // 8)
    return half, per, row_split


def piece_at(index, per, row_split, rows):
    first = index // row_split * per
    row = pl.multiple_of(lax.rem(index, row_split) * rows, 8) if row_split > 1 else 0
    return pl.ds(first, per), pl.ds(row, rows)


def loadings_kernel(
    load_chunks, early, pos_chunk,
    spectra, basis, loadings,
    new_loadings, nl2, s_hi, s_lo, tied3, packed,
    sbuf, own, other, load, tied2, num_out, num_in,
    sp_sem, io_sem, bs_sem, nm_sem,
):
    rank, pixels = basis.shape
    positions = loadings.shape[1]
    blocks = pixels // LANES
    pack = LANES // rank
    partner = {"det": 1 - lax.axis_index("det")}
    barrier = pltpu.get_barrier_semaphore()
    pl.semaphore_signal(barrier, inc=1, device_id=partner, device_id_type=MESH)

    load_rows = positions // load_chunks
    spectra_copies = []
    for i in range(load_chunks):
        part = pl.ds(i * load_rows, load_rows)
        spectra_copies.append(
            pltpu.make_async_copy(spectra.at[part], sbuf.at[part], sp_sem.at[i])
        )
    own_copy = pltpu.make_async_copy(basis, own, io_sem.at[0])
    load_copy = pltpu.make_async_copy(loadings, load, io_sem.at[1])
    basis_copy = remote(basis, other, bs_sem.at[0], bs_sem.at[1], partner)
    for i in range(early):
        spectra_copies[i].start()
    pl.semaphore_wait(barrier, 1)
    basis_copy.start()
    own_copy.start()
    load_copy.start()
    for i in range(early, load_chunks):
        spectra_copies[i].start()

    def divide(i):
        spectra_copies[i].wait()

        @pl.loop(0, load_rows // 16)
        def _(j):
            part = pl.ds(pl.multiple_of(i * load_rows + j * 16, 16), 16)
            hi, lo = split(sbuf[part, :])
            s_hi[part, :] = hi
            s_lo[part, :] = lo

    per_pos = pos_chunk // load_rows
    for i in range(early):
        divide(i)
    own_copy.wait()
    basis_copy.wait()
    for b in range(blocks):
        mine = own[:, b * LANES:(b + 1) * LANES]
        back = blocks - 1 - b
        tied = 0.5 * (mine + mirrored(other[:, back * LANES:(back + 1) * LANES]))
        tied3[b] = tied
        hi, lo = split(tied)
        tied2[:rank, b * LANES:(b + 1) * LANES] = hi
        tied2[rank:, b * LANES:(b + 1) * LANES] = lo

    chunks = positions // pos_chunk
    num_copies = [
        remote(num_out.at[i], num_in.at[i], nm_sem.at[0, i], nm_sem.at[1, i], partner)
        for i in range(chunks)
    ]

    def products(i):
        for j in range(max(i * per_pos, early), (i + 1) * per_pos):
            divide(j)
        part = pl.ds(i * pos_chunk, pos_chunk)
        both = dot_nt(tied2[...], s_hi[part, :])
        low = dot_nt(tied2[:rank, :], s_lo[part, :])
        num_out[i] = both[:rank] + (both[rank:] + low)
        num_copies[i].start()

    def update(i):
        num_copies[i].wait()
        cols = slice(i * pos_chunk, (i + 1) * pos_chunk)
        fresh = load[:, cols] * (num_out[i] + num_in[i]) / weighted[:, cols]
        new_loadings[:, cols] = fresh
        hi, lo = split(fresh)
        nl2[:rank, cols] = hi
        nl2[rank:, cols] = lo
        return dot_nt(nl2[:, cols], nl2[:, cols])

    products(0)
    squares = dot_nt(tied2[...], tied2[...])
    gram = 2.0 * (
        squares[:rank, :rank] + (squares[:rank, rank:] + squares[rank:, :rank])
    )
    load_copy.wait()
    weighted = jnp.dot(gram, load[...], precision=HIGHEST, preferred_element_type=F32)
    squares = 0.0
    for i in range(1, chunks):
        products(i)
        if i > 1:
            squares = squares + update(i - 2)
    for i in range(max(chunks - 2, 0), chunks):
        squares = squares + update(i)
    cross = squares[:rank, :rank] + (squares[:rank, rank:] + squares[rank:, :rank])
    packed[...] = jnp.concatenate(
        [cross[i * (rank // pack):(i + 1) * (rank // pack)] for i in range(pack)], axis=1
    )


def basis_kernel(
    n, col_chunk, wait_at,
    nl2, s_hi, s_lo, tied3, packed,
    piece_buf, ag_in, fw_in,
    w_keep, w_out, w_in, rs_in, cr_out, cr_in,
    io_sem, w_sem, rs_send, rs_recv, cr_send, cr_recv,
    ag_send, ag_recv, fw_send, fw_recv,
):
    blocks, rank, _ = tied3.shape
    half, per, row_split = layout(n, rank, blocks * LANES)
    owners = half // per * row_split
    rows = rank // row_split
    pack = LANES // rank
    me = lax.axis_index("scan")
    partner = {"det": 1 - lax.axis_index("det")}

    def peer(k):
        return lax.rem(me + k, n)

    def source(k):
        return lax.rem(me + n - k, n)

    def owner_only(index, fn):
        if owners == n:
            fn()
        else:
            pl.when(index < owners)(fn)

    barrier = pltpu.get_barrier_semaphore()
    for k in range(1, n):
        pl.semaphore_signal(barrier, inc=1, device_id={"scan": peer(k)}, device_id_type=MESH)
    pl.semaphore_signal(barrier, inc=1, device_id=partner, device_id_type=MESH)
    keep = pltpu.make_async_copy(packed, cr_out, io_sem.at[0])
    keep.start()

    def sums(cols):
        both = dot_nn(nl2[...], s_hi[:, cols])
        low = dot_nn(nl2[:rank, :], s_lo[:, cols])
        return both[:rank] + (both[rank:] + low)

    step = col_chunk // LANES
    count = half // step
    w_copies = []
    for i in range(count):
        part = pl.ds(i * step, step)
        w_copies.append(
            remote(w_out.at[part], w_in.at[part], w_sem.at[0, i], w_sem.at[1, i], partner)
        )
    cr_copies = [None]
    for k in range(1, n):
        cr_copies.append(
            remote(cr_out, cr_in.at[k], cr_send.at[k], cr_recv.at[k], {"scan": peer(k)})
        )
    for i in range(count):
        first = half + i * step
        value = sums(slice(first * LANES, (first + step) * LANES))
        for j in range(step):
            w_out[i * step + j] = value[:, j * LANES:(j + 1) * LANES]
    keep.wait()

    def meet():
        pl.semaphore_wait(barrier, n)
        for copy in w_copies:
            copy.start()
        for k in range(1, n):
            cr_copies[k].start()

    for i in range(count):
        if i == wait_at:
            meet()
        value = sums(slice(i * col_chunk, (i + 1) * col_chunk))
        for j in range(step):
            w_keep[i * step + j] = value[:, j * LANES:(j + 1) * LANES]
    if wait_at >= count:
        meet()
    for copy in w_copies:
        copy.wait()
    for b in range(half):
        w_keep[b] = w_keep[b] + mirrored(w_in[half - 1 - b])

    rs_copies = [None]
    for k in range(1, n):
        rs_copies.append(
            remote(
                w_keep.at[piece_at(peer(k), per, row_split, rows)], rs_in.at[k],
                rs_send.at[k], rs_recv.at[k], {"scan": peer(k)},
            )
        )
        owner_only(peer(k), rs_copies[k].start)

    for k in range(1, n):
        cr_copies[k].wait()
    total = cr_out[...]
    for k in range(1, n):
        total = total + cr_in[k]
    cross = jnp.concatenate(
        [total[:, i * rank:(i + 1) * rank] for i in range(pack)], axis=0
    )

    ag_copies = [None]
    for k in range(1, n):
        ag_copies.append(
            remote(piece_buf, ag_in.at[k], ag_send.at[k], ag_recv.at[k], {"scan": peer(k)})
        )
    fw_copies = [remote(piece_buf, fw_in.at[0], fw_send.at[0], fw_recv.at[0], partner)]
    for k in range(1, n):
        fw_copies.append(
            remote(ag_in.at[k], fw_in.at[k], fw_send.at[k], fw_recv.at[k], partner)
        )

    def own_piece():
        first, row = piece_at(me, per, row_split, rows)
        for j in range(per):
            weights = jnp.dot(
                cross, tied3[first.start + j], precision=HIGHEST, preferred_element_type=F32
            )
            if row_split > 1:
                piece_buf[0] = weights[:rows]
                for i in range(1, row_split):
                    @pl.when(lax.rem(me, row_split) == i)
                    def _():
                        piece_buf[0] = weights[i * rows:(i + 1) * rows]
            else:
                piece_buf[j] = weights
        for k in range(1, n):
            rs_copies[k].wait_recv()
        for j in range(per):
            total = w_keep[first.start + j, row, :]
            for k in range(1, n):
                total = total + rs_in[k, j]
            piece_buf[j] = tied3[first.start + j, row, :] * (0.5 * total) / piece_buf[j]
        for k in range(1, n):
            ag_copies[k].start()
        fw_copies[0].start()

    owner_only(me, own_piece)

    def arrived(k):
        def go():
            ag_copies[k].wait_recv()
            fw_copies[k].start()
        return go

    for k in range(1, n):
        owner_only(source(k), arrived(k))
    owner_only(me, fw_copies[0].wait)
    for k in range(1, n):
        owner_only(source(k), fw_copies[k].wait)
    for k in range(1, n):
        owner_only(peer(k), rs_copies[k].wait_send)
        owner_only(me, ag_copies[k].wait_send)


def output_kernel(
    n, fresh, piece_buf, ag_in, fw_in, new_loadings, new_basis, nb, io_sem
):
    rank, pixels = nb.shape
    half, per, row_split = layout(n, rank, pixels)
    owners = half // per * row_split
    rows = rank // row_split
    me = lax.axis_index("scan")
    first_copy = pltpu.make_async_copy(fresh, new_loadings, io_sem.at[0])
    first_copy.start()

    def put(index, ref, flip):
        first, row = piece_at(index, per, row_split, rows)
        for j in range(per):
            block = first.start + j
            value = ref[j]
            if flip:
                block = pixels // LANES - 1 - block
                value = mirrored(value)
            nb[row, pl.ds(pl.multiple_of(block * LANES, LANES), LANES)] = value

    for k in range(n):
        index = lax.rem(me + n - k, n)

        def go():
            put(index, piece_buf if k == 0 else ag_in.at[k], False)
            put(index, fw_in.at[k], True)

        if owners == n:
            go()
        else:
            pl.when(index < owners)(go)
    second_copy = pltpu.make_async_copy(nb, new_basis, io_sem.at[1])
    second_copy.start()
    first_copy.wait()
    second_copy.wait()


def per_device(n, spectra, basis, loadings):
    rank, pixels = basis.shape
    positions = loadings.shape[1]
    blocks = pixels // LANES
    half, per, row_split = layout(n, rank, pixels)
    rows = rank // row_split
    load_chunks = 8
    pos_chunk = positions // 4
    col_chunk = 2 * LANES
    pack = LANES // rank
    dma = pltpu.SemaphoreType.DMA
    any_space = pl.BlockSpec(memory_space=pl.ANY)
    vmem = pl.BlockSpec(memory_space=pltpu.VMEM)
    fresh, nl2, s_hi, s_lo, tied3, packed = pl.pallas_call(
        functools.partial(loadings_kernel, load_chunks, 4, pos_chunk),
        out_shape=(
            pltpu.VMEM(loadings.shape, F32),
            pltpu.VMEM((2 * rank, positions), BF16),
            pltpu.VMEM(spectra.shape, BF16),
            pltpu.VMEM(spectra.shape, BF16),
            pltpu.VMEM((blocks, rank, LANES), F32),
            pltpu.VMEM((rank // pack, LANES), F32),
        ),
        in_specs=[pl.BlockSpec(memory_space=pltpu.HBM)] * 3,
        out_specs=(vmem,) * 6,
        scratch_shapes=[
            pltpu.VMEM(spectra.shape, F32),
            pltpu.VMEM((rank, pixels), F32),
            pltpu.VMEM((rank, pixels), F32),
            pltpu.VMEM((rank, positions), F32),
            pltpu.VMEM((2 * rank, pixels), BF16),
            pltpu.VMEM((positions // pos_chunk, rank, pos_chunk), F32),
            pltpu.VMEM((positions // pos_chunk, rank, pos_chunk), F32),
            dma((load_chunks,)),
            dma((2,)),
            dma((2,)),
            dma((2, positions // pos_chunk)),
        ],
        compiler_params=pltpu.CompilerParams(
            collective_id=0, has_side_effects=True, vmem_limit_bytes=40 << 20
        ),
        name="loadings_update",
    )(spectra, basis, loadings)
    pieces = pl.pallas_call(
        functools.partial(basis_kernel, n, col_chunk, 3),
        out_shape=(
            pltpu.VMEM((per, rows, LANES), F32),
            pltpu.VMEM((n, per, rows, LANES), F32),
            pltpu.VMEM((n, per, rows, LANES), F32),
        ),
        in_specs=[vmem] * 5,
        out_specs=(vmem,) * 3,
        scratch_shapes=[
            pltpu.VMEM((half, rank, LANES), F32),
            pltpu.VMEM((half, rank, LANES), F32),
            pltpu.VMEM((half, rank, LANES), F32),
            pltpu.VMEM((n, per, rows, LANES), F32),
            pltpu.VMEM((rank // pack, LANES), F32),
            pltpu.VMEM((n, rank // pack, LANES), F32),
            dma((1,)),
            dma((2, half * LANES // col_chunk)),
            dma((n,)), dma((n,)), dma((n,)), dma((n,)),
            dma((n,)), dma((n,)), dma((n,)), dma((n,)),
        ],
        compiler_params=pltpu.CompilerParams(
            collective_id=1, has_side_effects=True, vmem_limit_bytes=32 << 20
        ),
        name="basis_update",
    )(nl2, s_hi, s_lo, tied3, packed)
    return pl.pallas_call(
        functools.partial(output_kernel, n),
        out_shape=(
            jax.ShapeDtypeStruct(loadings.shape, F32),
            jax.ShapeDtypeStruct(basis.shape, F32),
        ),
        in_specs=[vmem] * 4,
        out_specs=(any_space,) * 2,
        scratch_shapes=[pltpu.VMEM((rank, pixels), F32), dma((2,))],
        compiler_params=pltpu.CompilerParams(vmem_limit_bytes=8 << 20),
        name="write_out",
    )(fresh, *pieces)


def solution(mesh):
    in_specs = (P(("grp", "scan"), "det"), P("grp", "det"), P("grp", "scan"))
    out_specs = (P("grp", "scan"), P("grp", "det"))
    return jax.shard_map(
        functools.partial(per_device, mesh.shape["scan"]),
        mesh=mesh, in_specs=in_specs, out_specs=out_specs, check_vma=False,
    )
```

time: 32.9 us -> 31.9 us (0.970)
  local copies, waits for them, and re-layouts: 3.24 us -> 1.85 us
  Pallas kernels: 28.6 us -> 29.2 us
    unnamed x2 -> x4, local copies, waits for them, and re-layouts: 3.24 us -> 1.85 us
    pallas_call x1 -> x3, Pallas kernels: 28.6 us -> 29.2 us  [the longest x1 18.3 us: per_device(): pl.pallas_call(functools.partial(basis_kernel, n, col_chunk, 3), out_shap...]
where the time goes in v2:
time: 31.9 us; the launch traced here: 31.7 us
  Pallas kernels  29.2 us (92%)
  local copies, waits for them, and re-layouts  1.85 us (6%)
  between operations  0.66 us (2%)
    pallas_call x1, Pallas kernels, per_device(): pl.pallas_call(functools.partial(basis_kernel, n, col_chunk, 3), out_shap...  18.3 us
    pallas_call x1, Pallas kernels, per_device(): pl.pallas_call(functools.partial(loadings_kernel, load_chunks, 4, pos_chu...  10.2 us
    unnamed x4, local copies, waits for them, and re-layouts  1.85 us
    pallas_call x1, Pallas kernels, per_device(): pl.pallas_call(functools.partial(output_kernel, n), out_shape=(jax.ShapeD...  0.83 us

profile of v2, /device:TPU:0, one launch (start us, length us, event | category | flops | bytes accessed | tf_op | source)
XLA Modules:
  0.0 31.7 jit_solution(96977019723766693)
XLA Ops:
  0.6 0.0 copy-start
  0.6 0.9 %copy-done = f32[32,2048]{1,0:T(8,128)S(1)} copy-done((f32[32,2048]{1,0:T(8,128)S(1)}, f32[32,2048]{1,0:T(8,128)}, u32[]{:S(2)}) %copy-start) | copy-done | bytes 262168
  1.6 0.0 copy-start.1
  1.6 0.9 %copy-done.1 = f32[32,1024]{1,0:T(8,128)S(1)} copy-done((f32[32,1024]{1,0:T(8,128)S(1)}, f32[32,1024]{1,0:T(8,128)}, u32[]{:S(2)}) %copy-start.1) | copy-done | bytes 131096
  2.5 10.2 %loadings_update.1 = (f32[32,1024]{1,0:T(8,128)S(1)}, bf16[64,1024]{1,0:T(8,128)(2,1)S(1)}, bf16[1024,2048]{1,0:T(8,128)(2,1)S(1)}, bf16[1024,2048]{1,0:T(8,128)...) custom-call(f32[1024,2048]{1,0:T(8,128)} %spectra.1, f32[32,2048]{1,0:T(8,128)S(1)} %copy-done, ...), custom_call_target="tpu_custom_call" | custom-call | tf_op jit(solution)/shard_map/loadings_update/pallas_call | solution.py:365
  12.6 18.3 %basis_update.1 = (f32[1,32,128]{2,1,0:T(8,128)S(1)}, f32[8,1,32,128]{3,2,1,0:T(8,128)S(1)}, f32[8,1,32,128]{3,2,1,0:T(8,128)S(1)}) custom-call(bf16[64,1024]{1,0:T(8,128)(2,1)S(1)} %get-tuple-element.12.nl2, bf16[1024,2048]{1,0:T(8,128)(2,1)S(1)} %get-tuple-element.13.s_hi, bf16[1024,2048]{1,0:T(8,128)(2,1)S(1)} %get-tuple-element.14.s_lo, ...), custom_call_target="tpu_custom_call" | custom-call | tf_op jit(solution)/shard_map/basis_update/pallas_call | solution.py:395
  30.9 0.8 %write_out.1 = (f32[32,1024]{1,0:T(8,128)}, f32[32,2048]{1,0:T(8,128)}) custom-call(f32[32,1024]{1,0:T(8,128)S(1)} %get-tuple-element.11.fresh, f32[1,32,128]{2,1,0:T(8,128)S(1)} %get-tuple-element.17.piece_buf, f32[8,1,32,128]{3,2,1,0:T(8,128)S(1)} %get-tuple-element.18.ag_in, f32[8,1,32,128]{3,2,1,0:T(8,128)S(1)} %get-tuple-element.19.fw_in), custom_call_target="tpu_custom_call" | custom-call | tf_op jit(solution)/shard_map/write_out/pallas_call | solution.py:421
Async XLA Ops:
  0.6 1.0 %copy-start = (f32[32,2048]{1,0:T(8,128)S(1)}, f32[32,2048]{1,0:T(8,128)}, u32[]{:S(2)}) copy-start(f32[32,2048]{1,0:T(8,128)} %basis.1) | copy-start | bytes 786436
  1.6 0.9 %copy-start.1 = (f32[32,1024]{1,0:T(8,128)S(1)}, f32[32,1024]{1,0:T(8,128)}, u32[]{:S(2)}) copy-start(f32[32,1024]{1,0:T(8,128)} %loadings.1) | copy-start | bytes 393220

commit v3 on v2

--- a/solution.py
+++ b/solution.py
@@ -55,17 +55,15 @@
     return pl.ds(first, per), pl.ds(row, rows)
 
 
-def loadings_kernel(
-    load_chunks, early, pos_chunk,
+def tie_kernel(
+    load_chunks, early,
     spectra, basis, loadings,
-    new_loadings, nl2, s_hi, s_lo, tied3, packed,
-    sbuf, own, other, load, tied2, num_out, num_in,
-    sp_sem, io_sem, bs_sem, nm_sem,
+    s_hi, s_lo, tied3, tied2, load, weighted,
+    sbuf, own, other, sp_sem, io_sem, bs_sem,
 ):
     rank, pixels = basis.shape
     positions = loadings.shape[1]
     blocks = pixels // LANES
-    pack = LANES // rank
     partner = {"det": 1 - lax.axis_index("det")}
     barrier = pltpu.get_barrier_semaphore()
     pl.semaphore_signal(barrier, inc=1, device_id=partner, device_id_type=MESH)
@@ -92,14 +90,13 @@
     def divide(i):
         spectra_copies[i].wait()
 
-        @pl.loop(0, load_rows // 16)
+        @pl.loop(0, load_rows // 16, unroll=True)
         def _(j):
             part = pl.ds(pl.multiple_of(i * load_rows + j * 16, 16), 16)
             hi, lo = split(sbuf[part, :])
             s_hi[part, :] = hi
             s_lo[part, :] = lo
 
-    per_pos = pos_chunk // load_rows
     for i in range(early):
         divide(i)
     own_copy.wait()
@@ -112,58 +109,24 @@
         hi, lo = split(tied)
         tied2[:rank, b * LANES:(b + 1) * LANES] = hi
         tied2[rank:, b * LANES:(b + 1) * LANES] = lo
-
-    chunks = positions // pos_chunk
-    num_copies = [
-        remote(num_out.at[i], num_in.at[i], nm_sem.at[0, i], nm_sem.at[1, i], partner)
-        for i in range(chunks)
-    ]
-
-    def products(i):
-        for j in range(max(i * per_pos, early), (i + 1) * per_pos):
-            divide(j)
-        part = pl.ds(i * pos_chunk, pos_chunk)
-        both = dot_nt(tied2[...], s_hi[part, :])
-        low = dot_nt(tied2[:rank, :], s_lo[part, :])
-        num_out[i] = both[:rank] + (both[rank:] + low)
-        num_copies[i].start()
-
-    def update(i):
-        num_copies[i].wait()
-        cols = slice(i * pos_chunk, (i + 1) * pos_chunk)
-        fresh = load[:, cols] * (num_out[i] + num_in[i]) / weighted[:, cols]
-        new_loadings[:, cols] = fresh
-        hi, lo = split(fresh)
-        nl2[:rank, cols] = hi
-        nl2[rank:, cols] = lo
-        return dot_nt(nl2[:, cols], nl2[:, cols])
-
-    products(0)
     squares = dot_nt(tied2[...], tied2[...])
     gram = 2.0 * (
         squares[:rank, :rank] + (squares[:rank, rank:] + squares[rank:, :rank])
     )
     load_copy.wait()
-    weighted = jnp.dot(gram, load[...], precision=HIGHEST, preferred_element_type=F32)
-    squares = 0.0
-    for i in range(1, chunks):
-        products(i)
-        if i > 1:
-            squares = squares + update(i - 2)
-    for i in range(max(chunks - 2, 0), chunks):
-        squares = squares + update(i)
-    cross = squares[:rank, :rank] + (squares[:rank, rank:] + squares[rank:, :rank])
-    packed[...] = jnp.concatenate(
-        [cross[i * (rank // pack):(i + 1) * (rank // pack)] for i in range(pack)], axis=1
-    )
-
-
-def basis_kernel(
-    n, col_chunk, wait_at,
-    nl2, s_hi, s_lo, tied3, packed,
-    piece_buf, ag_in, fw_in,
-    w_keep, w_out, w_in, rs_in, cr_out, cr_in,
-    io_sem, w_sem, rs_send, rs_recv, cr_send, cr_recv,
+    weighted[...] = jnp.dot(
+        gram, load[...], precision=HIGHEST, preferred_element_type=F32
+    )
+    for i in range(early, load_chunks):
+        divide(i)
+
+
+def update_kernel(
+    n, pos_chunk, col_chunk, wait_at,
+    s_hi, s_lo, tied3, tied2, load, weighted,
+    new_loadings, piece_buf, ag_in, fw_in,
+    nl2, num_out, num_in, w_keep, w_out, w_in, rs_in, cr_out, cr_in,
+    nm_sem, w_sem, rs_send, rs_recv, cr_send, cr_recv,
     ag_send, ag_recv, fw_send, fw_recv,
 ):
     blocks, rank, _ = tied3.shape
@@ -190,8 +153,38 @@
     for k in range(1, n):
         pl.semaphore_signal(barrier, inc=1, device_id={"scan": peer(k)}, device_id_type=MESH)
     pl.semaphore_signal(barrier, inc=1, device_id=partner, device_id_type=MESH)
-    keep = pltpu.make_async_copy(packed, cr_out, io_sem.at[0])
-    keep.start()
+    positions = load.shape[1]
+    chunks = positions // pos_chunk
+    num_copies = [
+        remote(num_out.at[i], num_in.at[i], nm_sem.at[0, i], nm_sem.at[1, i], partner)
+        for i in range(chunks)
+    ]
+
+    def products(i):
+        part = pl.ds(i * pos_chunk, pos_chunk)
+        both = dot_nt(tied2[...], s_hi[part, :])
+        low = dot_nt(tied2[:rank, :], s_lo[part, :])
+        num_out[i] = both[:rank] + (both[rank:] + low)
+
+    def update(i):
+        num_copies[i].wait()
+        cols = slice(i * pos_chunk, (i + 1) * pos_chunk)
+        fresh = load[:, cols] * (num_out[i] + num_in[i]) / weighted[:, cols]
+        new_loadings[:, cols] = fresh
+        hi, lo = split(fresh)
+        nl2[:rank, cols] = hi
+        nl2[rank:, cols] = lo
+
+    for i in range(chunks):
+        products(i)
+        if i == wait_at:
+            pl.semaphore_wait(barrier, n)
+            for j in range(i):
+                num_copies[j].start()
+        if i >= wait_at:
+            num_copies[i].start()
+    for i in range(chunks):
+        update(i)
 
     def sums(cols):
         both = dot_nn(nl2[...], s_hi[:, cols])
@@ -216,23 +209,19 @@
         value = sums(slice(first * LANES, (first + step) * LANES))
         for j in range(step):
             w_out[i * step + j] = value[:, j * LANES:(j + 1) * LANES]
-    keep.wait()
-
-    def meet():
-        pl.semaphore_wait(barrier, n)
-        for copy in w_copies:
-            copy.start()
-        for k in range(1, n):
-            cr_copies[k].start()
+        w_copies[i].start()
+    squares = dot_nt(nl2[...], nl2[...])
+    cross = squares[:rank, :rank] + (squares[:rank, rank:] + squares[rank:, :rank])
+    cr_out[...] = jnp.concatenate(
+        [cross[i * (rank // pack):(i + 1) * (rank // pack)] for i in range(pack)], axis=1
+    )
+    for k in range(1, n):
+        cr_copies[k].start()
 
     for i in range(count):
-        if i == wait_at:
-            meet()
         value = sums(slice(i * col_chunk, (i + 1) * col_chunk))
         for j in range(step):
             w_keep[i * step + j] = value[:, j * LANES:(j + 1) * LANES]
-    if wait_at >= count:
-        meet()
     for copy in w_copies:
         copy.wait()
     for b in range(half):
@@ -362,53 +351,54 @@
     dma = pltpu.SemaphoreType.DMA
     any_space = pl.BlockSpec(memory_space=pl.ANY)
     vmem = pl.BlockSpec(memory_space=pltpu.VMEM)
-    fresh, nl2, s_hi, s_lo, tied3, packed = pl.pallas_call(
-        functools.partial(loadings_kernel, load_chunks, 4, pos_chunk),
+    hbm = pl.BlockSpec(memory_space=pltpu.HBM)
+    inputs = [pltpu.with_memory_space_constraint(x, pltpu.HBM) for x in (spectra, basis, loadings)]
+    parts = pl.pallas_call(
+        functools.partial(tie_kernel, load_chunks, 4),
         out_shape=(
-            pltpu.VMEM(loadings.shape, F32),
-            pltpu.VMEM((2 * rank, positions), BF16),
             pltpu.VMEM(spectra.shape, BF16),
             pltpu.VMEM(spectra.shape, BF16),
             pltpu.VMEM((blocks, rank, LANES), F32),
-            pltpu.VMEM((rank // pack, LANES), F32),
+            pltpu.VMEM((2 * rank, pixels), BF16),
+            pltpu.VMEM((rank, positions), F32),
+            pltpu.VMEM((rank, positions), F32),
         ),
-        in_specs=[pl.BlockSpec(memory_space=pltpu.HBM)] * 3,
+        in_specs=[hbm] * 3,
         out_specs=(vmem,) * 6,
         scratch_shapes=[
             pltpu.VMEM(spectra.shape, F32),
             pltpu.VMEM((rank, pixels), F32),
             pltpu.VMEM((rank, pixels), F32),
-            pltpu.VMEM((rank, positions), F32),
-            pltpu.VMEM((2 * rank, pixels), BF16),
-            pltpu.VMEM((positions // pos_chunk, rank, pos_chunk), F32),
-            pltpu.VMEM((positions // pos_chunk, rank, pos_chunk), F32),
             dma((load_chunks,)),
             dma((2,)),
             dma((2,)),
-            dma((2, positions // pos_chunk)),
         ],
         compiler_params=pltpu.CompilerParams(
-            collective_id=0, has_side_effects=True, vmem_limit_bytes=40 << 20
+            collective_id=0, has_side_effects=True, vmem_limit_bytes=32 << 20
         ),
-        name="loadings_update",
-    )(spectra, basis, loadings)
-    pieces = pl.pallas_call(
-        functools.partial(basis_kernel, n, col_chunk, 3),
+        name="tie_and_split",
+    )(*inputs)
+    outs = pl.pallas_call(
+        functools.partial(update_kernel, n, pos_chunk, col_chunk, 2),
         out_shape=(
+            pltpu.VMEM(loadings.shape, F32),
             pltpu.VMEM((per, rows, LANES), F32),
             pltpu.VMEM((n, per, rows, LANES), F32),
             pltpu.VMEM((n, per, rows, LANES), F32),
         ),
-        in_specs=[vmem] * 5,
-        out_specs=(vmem,) * 3,
+        in_specs=[vmem] * 6,
+        out_specs=(vmem,) * 4,
         scratch_shapes=[
+            pltpu.VMEM((2 * rank, positions), BF16),
+            pltpu.VMEM((positions // pos_chunk, rank, pos_chunk), F32),
+            pltpu.VMEM((positions // pos_chunk, rank, pos_chunk), F32),
             pltpu.VMEM((half, rank, LANES), F32),
             pltpu.VMEM((half, rank, LANES), F32),
             pltpu.VMEM((half, rank, LANES), F32),
             pltpu.VMEM((n, per, rows, LANES), F32),
             pltpu.VMEM((rank // pack, LANES), F32),
             pltpu.VMEM((n, rank // pack, LANES), F32),
-            dma((1,)),
+            dma((2, positions // pos_chunk)),
             dma((2, half * LANES // col_chunk)),
             dma((n,)), dma((n,)), dma((n,)), dma((n,)),
             dma((n,)), dma((n,)), dma((n,)), dma((n,)),
@@ -416,8 +406,8 @@
         compiler_params=pltpu.CompilerParams(
             collective_id=1, has_side_effects=True, vmem_limit_bytes=32 << 20
         ),
-        name="basis_update",
-    )(nl2, s_hi, s_lo, tied3, packed)
+        name="update",
+    )(*parts)
     return pl.pallas_call(
         functools.partial(output_kernel, n),
         out_shape=(
@@ -429,7 +419,7 @@
         scratch_shapes=[pltpu.VMEM((rank, pixels), F32), dma((2,))],
         compiler_params=pltpu.CompilerParams(vmem_limit_bytes=8 << 20),
         name="write_out",
-    )(fresh, *pieces)
+    )(*outs)
 
 
 def solution(mesh):

time: 31.9 us -> 28.6 us (0.90)
  local copies, waits for them, and re-layouts: 1.85 us -> 0 us
  Pallas kernels: 29.2 us -> 27.8 us
    unnamed x4 -> x0, local copies, waits for them, and re-layouts: 1.85 us -> none
    pallas_call x2, Pallas kernels: 28.4 us -> 26.9 us  [the longest x1 22.6 us: per_device(): pl.pallas_call(functools.partial(update_kernel, n, pos_chunk, col_chunk,...]
where the time goes in v3:
time: 28.6 us; the launch traced here: 28.4 us
  Pallas kernels  27.8 us (97%)
  between operations  0.65 us (2%)
    pallas_call x1, Pallas kernels, per_device(): pl.pallas_call(functools.partial(update_kernel, n, pos_chunk, col_chunk,...  22.6 us
    pallas_call x1, Pallas kernels, per_device(): pl.pallas_call(functools.partial(tie_kernel, load_chunks, 4), out_shape=(...  4.38 us
    pallas_call x1, Pallas kernels, per_device(): pl.pallas_call(functools.partial(output_kernel, n), out_shape=(jax.ShapeD...  0.83 us

profile of v3, /device:TPU:0, one launch (start us, length us, event | category | flops | bytes accessed | tf_op | source)
XLA Modules:
  0.0 28.4 jit_solution(7307451294716956150)
XLA Ops:
  0.6 4.4 %tie_and_split.1 = (bf16[1024,2048]{1,0:T(8,128)(2,1)S(1)}, bf16[1024,2048]{1,0:T(8,128)(2,1)S(1)}, f32[16,32,128]{2,1,0:T(8,128)S(1)}, bf16[64,2048]{1,0:T(8,12...) custom-call(f32[1024,2048]{1,0:T(8,128)} %spectra.1, f32[32,2048]{1,0:T(8,128)} %basis.1, f32[32,1024]{1,0:T(8,128)} %loadings.1), custom_call_target="tpu_custom_call" | custom-call | tf_op jit(solution)/shard_map/tie_and_split/pallas_call | solution.py:356
  5.0 22.6 %update.1 = (f32[32,1024]{1,0:T(8,128)S(1)}, f32[1,32,128]{2,1,0:T(8,128)S(1)}, f32[8,1,32,128]{3,2,1,0:T(8,128)S(1)}, f32[8,1,32,128]{3,2,1,0:T(8,128)S(1)}) custom-call(bf16[1024,2048]{1,0:T(8,128)(2,1)S(1)} %get-tuple-element.12.s_hi, bf16[1024,2048]{1,0:T(8,128)(2,1)S(1)} %get-tuple-element.13.s_lo, f32[16,32,128]{2,1,0:T(8,128)S(1)} %get-tuple-element.14.tied3, ...), custom_call_target="tpu_custom_call" | custom-call | tf_op jit(solution)/shard_map/update/pallas_call | solution.py:381
  27.6 0.8 %write_out.1 = (f32[32,1024]{1,0:T(8,128)}, f32[32,2048]{1,0:T(8,128)}) custom-call(f32[32,1024]{1,0:T(8,128)S(1)} %get-tuple-element.18.fresh, f32[1,32,128]{2,1,0:T(8,128)S(1)} %get-tuple-element.19.piece_buf, f32[8,1,32,128]{3,2,1,0:T(8,128)S(1)} %get-tuple-element.20.ag_in, f32[8,1,32,128]{3,2,1,0:T(8,128)S(1)} %get-tuple-element.21.fw_in), custom_call_target="tpu_custom_call" | custom-call | tf_op jit(solution)/shard_map/write_out/pallas_call | solution.py:411

commit v4 on v3

--- a/solution.py
+++ b/solution.py
@@ -153,6 +153,10 @@
     for k in range(1, n):
         pl.semaphore_signal(barrier, inc=1, device_id={"scan": peer(k)}, device_id_type=MESH)
     pl.semaphore_signal(barrier, inc=1, device_id=partner, device_id_type=MESH)
+    for k in range(1, n):
+        pl.semaphore_signal(
+            barrier, inc=1, device_id={"scan": peer(k), **partner}, device_id_type=MESH
+        )
     positions = load.shape[1]
     chunks = positions // pos_chunk
     num_copies = [
@@ -162,9 +166,9 @@
 
     def products(i):
         part = pl.ds(i * pos_chunk, pos_chunk)
-        both = dot_nt(tied2[...], s_hi[part, :])
-        low = dot_nt(tied2[:rank, :], s_lo[part, :])
-        num_out[i] = both[:rank] + (both[rank:] + low)
+        both = dot_nt(s_hi[part, :], tied2[...])
+        low = dot_nt(s_lo[part, :], tied2[:rank, :])
+        num_out[i] = (both[:, :rank] + (both[:, rank:] + low)).T
 
     def update(i):
         num_copies[i].wait()
@@ -178,7 +182,7 @@
     for i in range(chunks):
         products(i)
         if i == wait_at:
-            pl.semaphore_wait(barrier, n)
+            pl.semaphore_wait(barrier, 2 * n - 1)
             for j in range(i):
                 num_copies[j].start()
         if i >= wait_at:
@@ -254,7 +258,10 @@
     fw_copies = [remote(piece_buf, fw_in.at[0], fw_send.at[0], fw_recv.at[0], partner)]
     for k in range(1, n):
         fw_copies.append(
-            remote(ag_in.at[k], fw_in.at[k], fw_send.at[k], fw_recv.at[k], partner)
+            remote(
+                piece_buf, fw_in.at[k], fw_send.at[k], fw_recv.at[k],
+                {"scan": peer(k), **partner},
+            )
         )
 
     def own_piece():
@@ -280,6 +287,7 @@
             piece_buf[j] = tied3[first.start + j, row, :] * (0.5 * total) / piece_buf[j]
         for k in range(1, n):
             ag_copies[k].start()
+            fw_copies[k].start()
         fw_copies[0].start()
 
     owner_only(me, own_piece)
@@ -287,17 +295,17 @@
     def arrived(k):
         def go():
             ag_copies[k].wait_recv()
-            fw_copies[k].start()
         return go
 
     for k in range(1, n):
         owner_only(source(k), arrived(k))
     owner_only(me, fw_copies[0].wait)
     for k in range(1, n):
-        owner_only(source(k), fw_copies[k].wait)
+        owner_only(source(k), fw_copies[k].wait_recv)
     for k in range(1, n):
         owner_only(peer(k), rs_copies[k].wait_send)
         owner_only(me, ag_copies[k].wait_send)
+        owner_only(me, fw_copies[k].wait_send)
 
 
 def output_kernel(
@@ -345,8 +353,8 @@
     half, per, row_split = layout(n, rank, pixels)
     rows = rank // row_split
     load_chunks = 8
-    pos_chunk = positions // 4
-    col_chunk = 2 * LANES
+    pos_chunk = positions // 2
+    col_chunk = 4 * LANES
     pack = LANES // rank
     dma = pltpu.SemaphoreType.DMA
     any_space = pl.BlockSpec(memory_space=pl.ANY)
@@ -379,7 +387,7 @@
         name="tie_and_split",
     )(*inputs)
     outs = pl.pallas_call(
-        functools.partial(update_kernel, n, pos_chunk, col_chunk, 2),
+        functools.partial(update_kernel, n, pos_chunk, col_chunk, 1),
         out_shape=(
             pltpu.VMEM(loadings.shape, F32),
             pltpu.VMEM((per, rows, LANES), F32),

time: 28.6 us -> 26.3 us (0.920)
  Pallas kernels: 27.8 us -> 25.5 us
    pallas_call x1, Pallas kernels: 22.6 us -> 20.3 us  [per_device(): pl.pallas_call(functools.partial(update_kernel, n, pos_chunk, col_chunk,...]
where the time goes in v4:
time: 26.3 us; the launch traced here: 26.1 us
  Pallas kernels  25.5 us (97%)
  between operations  0.65 us (2%)
    pallas_call x1, Pallas kernels, per_device(): pl.pallas_call(functools.partial(update_kernel, n, pos_chunk, col_chunk,...  20.3 us
    pallas_call x1, Pallas kernels, per_device(): pl.pallas_call(functools.partial(tie_kernel, load_chunks, 4), out_shape=(...  4.38 us
    pallas_call x1, Pallas kernels, per_device(): pl.pallas_call(functools.partial(output_kernel, n), out_shape=(jax.ShapeD...  0.83 us

profile of v4, /device:TPU:0, one launch (start us, length us, event | category | flops | bytes accessed | tf_op | source)
XLA Modules:
  0.0 26.1 jit_solution(4948449333018091323)
XLA Ops:
  0.6 4.4 %tie_and_split.1 = (bf16[1024,2048]{1,0:T(8,128)(2,1)S(1)}, bf16[1024,2048]{1,0:T(8,128)(2,1)S(1)}, f32[16,32,128]{2,1,0:T(8,128)S(1)}, bf16[64,2048]{1,0:T(8,12...) custom-call(f32[1024,2048]{1,0:T(8,128)} %spectra.1, f32[32,2048]{1,0:T(8,128)} %basis.1, f32[32,1024]{1,0:T(8,128)} %loadings.1), custom_call_target="tpu_custom_call" | custom-call | tf_op jit(solution)/shard_map/tie_and_split/pallas_call | solution.py:364
  5.0 20.3 %update.1 = (f32[32,1024]{1,0:T(8,128)S(1)}, f32[1,32,128]{2,1,0:T(8,128)S(1)}, f32[8,1,32,128]{3,2,1,0:T(8,128)S(1)}, f32[8,1,32,128]{3,2,1,0:T(8,128)S(1)}) custom-call(bf16[1024,2048]{1,0:T(8,128)(2,1)S(1)} %get-tuple-element.12.s_hi, bf16[1024,2048]{1,0:T(8,128)(2,1)S(1)} %get-tuple-element.13.s_lo, f32[16,32,128]{2,1,0:T(8,128)S(1)} %get-tuple-element.14.tied3, ...), custom_call_target="tpu_custom_call" | custom-call | tf_op jit(solution)/shard_map/update/pallas_call | solution.py:389
  25.3 0.8 %write_out.1 = (f32[32,1024]{1,0:T(8,128)}, f32[32,2048]{1,0:T(8,128)}) custom-call(f32[32,1024]{1,0:T(8,128)S(1)} %get-tuple-element.18.fresh, f32[1,32,128]{2,1,0:T(8,128)S(1)} %get-tuple-element.19.piece_buf, f32[8,1,32,128]{3,2,1,0:T(8,128)S(1)} %get-tuple-element.20.ag_in, f32[8,1,32,128]{3,2,1,0:T(8,128)S(1)} %get-tuple-element.21.fw_in), custom_call_target="tpu_custom_call" | custom-call | tf_op jit(solution)/shard_map/write_out/pallas_call | solution.py:419

commit v5 on v4

--- a/solution.py
+++ b/solution.py
@@ -354,7 +354,7 @@
     rows = rank // row_split
     load_chunks = 8
     pos_chunk = positions // 2
-    col_chunk = 4 * LANES
+    col_chunk = 8 * LANES
     pack = LANES // rank
     dma = pltpu.SemaphoreType.DMA
     any_space = pl.BlockSpec(memory_space=pl.ANY)
@@ -362,7 +362,7 @@
     hbm = pl.BlockSpec(memory_space=pltpu.HBM)
     inputs = [pltpu.with_memory_space_constraint(x, pltpu.HBM) for x in (spectra, basis, loadings)]
     parts = pl.pallas_call(
-        functools.partial(tie_kernel, load_chunks, 4),
+        functools.partial(tie_kernel, load_chunks, 6),
         out_shape=(
             pltpu.VMEM(spectra.shape, BF16),
             pltpu.VMEM(spectra.shape, BF16),

time: 26.3 us -> 26 us (0.989)
  Pallas kernels: 25.5 us -> 25.2 us
where the time goes in v5:
time: 26 us; the launch traced here: 25.8 us
  Pallas kernels  25.2 us (97%)
  between operations  0.65 us (2%)
    pallas_call x1, Pallas kernels, per_device(): pl.pallas_call(functools.partial(update_kernel, n, pos_chunk, col_chunk,...  20.2 us
    pallas_call x1, Pallas kernels, per_device(): pl.pallas_call(functools.partial(tie_kernel, load_chunks, 6), out_shape=(...  4.13 us
    pallas_call x1, Pallas kernels, per_device(): pl.pallas_call(functools.partial(output_kernel, n), out_shape=(jax.ShapeD...  0.83 us

profile of v5, /device:TPU:0, one launch (start us, length us, event | category | flops | bytes accessed | tf_op | source)
XLA Modules:
  0.0 25.8 jit_solution(16694446272930369791)
XLA Ops:
  0.6 4.1 %tie_and_split.1 = (bf16[1024,2048]{1,0:T(8,128)(2,1)S(1)}, bf16[1024,2048]{1,0:T(8,128)(2,1)S(1)}, f32[16,32,128]{2,1,0:T(8,128)S(1)}, bf16[64,2048]{1,0:T(8,12...) custom-call(f32[1024,2048]{1,0:T(8,128)} %spectra.1, f32[32,2048]{1,0:T(8,128)} %basis.1, f32[32,1024]{1,0:T(8,128)} %loadings.1), custom_call_target="tpu_custom_call" | custom-call | tf_op jit(solution)/shard_map/tie_and_split/pallas_call | solution.py:364
  4.8 20.2 %update.1 = (f32[32,1024]{1,0:T(8,128)S(1)}, f32[1,32,128]{2,1,0:T(8,128)S(1)}, f32[8,1,32,128]{3,2,1,0:T(8,128)S(1)}, f32[8,1,32,128]{3,2,1,0:T(8,128)S(1)}) custom-call(bf16[1024,2048]{1,0:T(8,128)(2,1)S(1)} %get-tuple-element.12.s_hi, bf16[1024,2048]{1,0:T(8,128)(2,1)S(1)} %get-tuple-element.13.s_lo, f32[16,32,128]{2,1,0:T(8,128)S(1)} %get-tuple-element.14.tied3, ...), custom_call_target="tpu_custom_call" | custom-call | tf_op jit(solution)/shard_map/update/pallas_call | solution.py:389
  25.0 0.8 %write_out.1 = (f32[32,1024]{1,0:T(8,128)}, f32[32,2048]{1,0:T(8,128)}) custom-call(f32[32,1024]{1,0:T(8,128)S(1)} %get-tuple-element.18.fresh, f32[1,32,128]{2,1,0:T(8,128)S(1)} %get-tuple-element.19.piece_buf, f32[8,1,32,128]{3,2,1,0:T(8,128)S(1)} %get-tuple-element.20.ag_in, f32[8,1,32,128]{3,2,1,0:T(8,128)S(1)} %get-tuple-element.21.fw_in), custom_call_target="tpu_custom_call" | custom-call | tf_op jit(solution)/shard_map/write_out/pallas_call | solution.py:419
